TPU v7x, 256 devices: a whole 4x4x8 slice. The times are simulated.
256 devices in a mesh: win: 32 (over z_hi, y, core), chan: 8 (over z_lo, x).
Axes of the slice: x: 4, y: 4, z: 8 (z_hi: 4, z_lo: 2; z = z_hi * 2 + z_lo), core: 2. Of those that a mesh axis runs over, the one named last changes fastest.
Arguments:
- traces: bfloat16 [64, 2048, 4096], P('win', 'chan'), may hold values from -120 to 120
- block_pairs: int32 [32, 2], replicated, may hold values from 0 to 15
- valid_count: int32 [1], replicated, may hold values from 8 to 31
Outputs:
- cross_spectra: float32 [32, 8, 2, 128, 128], P('win', 'chan')
Inputs may be any that keep to these rules, and one draw needn't show every extreme that they name: `block_pairs`: entries are channel block numbers; a pair may repeat.
All inputs are finite; a program needn't handle non-finite values.
Results may differ from a plain program's by a relative error of at most 0.0037.
Values may be sent and summed in bfloat16 or wider, within the bound.
No kernel may reach another device: no remote copies, remote signals or barrier semaphores. Data moves between devices by JAX's collectives and lax.ppermute only.
A program may use at most 64 MiB of HBM per device.

v0:
```python
import math
import jax
import jax.numpy as jnp
from jax import lax
from jax.sharding import PartitionSpec as P

BLOCK = 128
NBINS = 256
FREQ_LO = 64
GROUP = 32
EPS = 1e-06


def dft_table(length, first_bin, bins):
    times = jnp.arange(length, dtype=jnp.int32)
    freqs = first_bin + jnp.arange(bins, dtype=jnp.int32)
    phases = times[:, None] * freqs[None, :] % length
    angles = phases.astype(jnp.float32) * (2.0 * math.pi / length)
    factor = 1.0 / math.sqrt(length)
    return (jnp.concatenate([jnp.cos(angles), -jnp.sin(angles)], axis=1) * factor).astype(
        jnp.bfloat16
    )


def block_layout(band_part, block, group):
    windows, channels, _, width = band_part.shape
    shaped = band_part.reshape(windows, channels // block, block, 2, width // group, group)
    rotated = jnp.stack([shaped[:, :, :, 1], -shaped[:, :, :, 0]], axis=3)

    def arrange(values):
        moved = jnp.transpose(values, (1, 4, 2, 0, 3, 5))
        return moved.reshape(channels // block, width // group, block, windows * 2 * group)

    return (arrange(shaped), arrange(rotated))


def pair_products(upper_direct, upper_rotated, lower):
    upper = jnp.concatenate([upper_direct, upper_rotated], axis=2)
    products = jnp.einsum("pgik,pgjk->pgij", upper, lower, preferred_element_type=jnp.float32)
    return products.reshape(products.shape[0], products.shape[1], 2, lower.shape[2], lower.shape[2])


def pair_terms(direct, rotated, chosen):
    return pair_products(direct[chosen[:, 0]], rotated[chosen[:, 0]], direct[chosen[:, 1]])


def on_device(traces, block_pairs, valid_count):
    windows, channels, length = traces.shape
    spectra = jnp.dot(
        traces.reshape(windows * channels, length),
        dft_table(length, FREQ_LO, NBINS),
        preferred_element_type=jnp.float32,
    )
    energy = jnp.sum(spectra * spectra, axis=1, keepdims=True) / NBINS
    whitened = (
        (spectra * lax.rsqrt(energy + EPS))
        .astype(jnp.bfloat16)
        .reshape(windows, channels, 2, NBINS)
    )
    banded = lax.all_to_all(whitened, "chan", split_axis=3, concat_axis=1, tiled=True)
    stack_scale = 1.0 / math.sqrt(windows * lax.axis_size("win") * GROUP)
    slots = block_pairs.shape[0] // lax.axis_size("win")
    first_slot = lax.axis_index("win") * slots
    mine = lax.dynamic_slice_in_dim(block_pairs, first_slot, slots, 0)
    direct, rotated = block_layout(lax.all_gather(banded, "win", axis=0, tiled=True), BLOCK, GROUP)
    stacked = pair_terms(direct, rotated, mine)
    slot_ids = first_slot + jnp.arange(slots, dtype=jnp.int32)
    live = (slot_ids < valid_count[0]).astype(jnp.float32)
    return stacked * stack_scale * live[:, None, None, None, None]


def solution(mesh):
    in_specs = (P("win", "chan", None), P(), P())
    out_specs = P("win", "chan", None, None, None)
    return jax.shard_map(
        on_device, mesh=mesh, in_specs=in_specs, out_specs=out_specs, check_vma=False
    )
```

profile of v0, /device:TPU:43, one launch (start us, length us, event | category | flops | bytes accessed | tf_op | source)
XLA Modules:
  0.0 213.0 jit_solution(3849331905427035691)
XLA Ops:
  6.5 0.0 copy-start
  6.5 0.0 all-gather.2.cloned.1.call-start
  6.5 0.0 copy-start.2
  6.5 16.7 %fusion.10 = (f32[4096,256]{1,0:T(8,128)S(1)}, f32[4096,256]{1,0:T(8,128)S(1)}) fusion(s32[256]{0:T(256)S(1)} %iota_add_fusion), kind=kLoop, calls=%fused_computation.17 | loop fusion | flops 15728640 | bytes 8389632 | tf_op jit(solution)/shard_map/cos | solution.py:20
  23.3 0.0 copy-done.2
  23.3 2.5 %multiply_reduce_fusion = (f32[512]{0:T(512)S(1)}, f32[512,512]{1,0:T(8,128)S(1)}) fusion(bf16[512,4096]{1,0:T(8,128)(2,1)S(1)} %bitcast.49, f32[4096,256]{1,0:T(8,128)S(1)} %get-tuple-element.43, f32[4096,256]{1,0:T(8,128)S(1)} %get-tuple-element.42), kind=kOutput, calls=%fused_computation.23 | convolution fusion | flops 2154298880 | bytes 13633536 | tf_op jit(solution)/shard_map/dot_general | solution.py:49
  25.8 0.1 fusion.14
  25.9 0.1 reshape.48
  26.0 0.8 copy.21
  26.8 12.4 %all_to_all.18 = bf16[2,256,2,256]{1,2,0,3:T(2,128)(2,1)S(1)} all-to-all(bf16[2,256,2,256]{1,2,0,3:T(2,128)(2,1)S(1)} %copy.21), channel_id=1, replica_groups=mesh['win'=32,'chan'=8] {'chan'}, dimensions={3} | all-to-all | bytes 1048576 | tf_op jit(solution)/shard_map/all_to_all | solution.py:60
  39.3 0.1 copy.22
  39.3 0.9 copy.28
  40.2 0.0 all-gather.2.cloned.1.call-update
  40.2 0.0 copy-done
  40.2 0.1 constant_dynamic-slice_fusion.2
  40.3 0.5 fusion.19
  45.1 116.9 %all-gather.2.cloned.1.call-done = bf16[64,2048,2,32]{1,3,2,0:T(8,128)(2,1)} async-done(((bf16[2,2048,2,32]{1,3,2,0:T(8,128)(2,1)}), bf16[64,2048,2,32]{1,3,2,0:T(8,128)(2,1)}) %all-gather.2.cloned.1.call-update) | async-done | bytes 16777232 | tf_op jit(solution)/shard_map/all_gather | solution.py:65
  162.0 9.6 %copy.29 = bf16[512,8,16,128]{3,2,1,0:T(8,128)(2,1)S(1)} copy(bf16[512,8,16,128]{3,1,2,0:T(8,128)(2,1)} %bitcast.45) | data formatting | bytes 33554432
  171.7 12.0 %copy.24 = bf16[16,1,128,64,2,32]{2,5,4,3,0,1:T(8,128)(2,1)} copy(bf16[16,1,128,64,2,32]{2,0,5,4,3,1:T(8,128)(2,1)S(1)} %bitcast.40) | data formatting | bytes 33554432 | tf_op jit(solution)/shard_map/transpose | solution.py:31
  183.6 1.7 fusion.18
  185.3 1.7 maximum_bitcast_fusion
  187.0 10.7 %copy.25 = bf16[16,1,128,64,2,32]{2,5,4,3,0,1:T(8,128)(2,1)S(1)} copy(bf16[16,1,128,64,2,32]{2,0,5,4,3,1:T(8,128)(2,1)S(1)} %maximum_bitcast_fusion) | data formatting | bytes 33554432 | tf_op jit(solution)/shard_map/transpose | solution.py:31
  197.7 1.4 constant_dynamic-slice_fusion
  199.0 0.0 copy-start.1
  199.0 1.6 pad_maximum_fusion
  200.6 2.9 %copy.26 = bf16[1,1,256,4096]{3,2,1,0:T(8,128)(2,1)S(1)} copy(bf16[1,1,256,4096]{2,3,0,1:T(8,128)(2,1)} %pad_maximum_fusion) | data formatting | bytes 4194304 | tf_op jit(solution)/shard_map/concatenate | solution.py:38
  203.5 2.6 %fusion.11 = f32[1,1,2,128,128]{4,3,2,1,0:T(8,128)} fusion(bf16[2,128,4096]{2,1,0:T(8,128)(2,1)S(1)} %bitcast.46, bf16[16,1,128,4096]{2,3,0,1:T(8,128)(2,1)} %bitcast.43, s32[]{:T(128)} %bitcast.12, f32[]{:T(128)} %bitcast.16), kind=kOutput, calls=%fused_computation.19 | convolution fusion | flops 268468224 | bytes 3277824 | tf_op jit(solution)/shard_map/pgik,pgjk->pgij/dot_general | solution.py:39
  206.2 0.0 copy-done.1
  (2 shorter events, 0.0 us)
Async XLA Ops:
  6.5 33.7 %copy-start = (s32[32,2]{0,1:T(2,128)S(1)}, s32[32,2]{0,1:T(2,128)}, u32[]{:S(2)}) copy-start(s32[32,2]{0,1:T(2,128)} %param.4) | copy-start | bytes 772
  6.5 155.5 %all-gather.2.cloned.1.call-start = ((), (), s32[]{:S(2)}) async-start(), calls=%async_computation.1 | async-start | bytes 17301504 | tf_op jit(solution)/shard_map/all_gather | solution.py:65
  6.5 16.7 %copy-start.2 = (bf16[2,256,4096]{2,1,0:T(8,128)(2,1)S(1)}, bf16[2,256,4096]{2,1,0:T(8,128)(2,1)}, u32[]{:S(2)}) copy-start(bf16[2,256,4096]{2,1,0:T(8,128)(2,1)} %param.3) | copy-start | bytes 12582916
  199.0 7.1 %copy-start.1 = (s32[32,2]{0,1:T(2,128)S(1)}, s32[32,2]{0,1:T(2,128)}, u32[]{:S(2)}) copy-start(s32[32,2]{0,1:T(2,128)} %param.4) | copy-start | bytes 772
Sparse Core Ops, SparseCore 0:
  40.4 121.6 all-gather.1
where the time goes:
time: 213 us
  waiting for transfers between devices  117 us (55%)
  local copies, waits for them, and re-layouts  39 us (18%)
  other arithmetic  21.8 us (10%)
  between operations  17.8 us (8%)
  blocking collectives  12.4 us (6%)
  matrix products  5.11 us (2%)
    all_gather x1, waiting for transfers between devices, on_device(): lax.all_gather(banded, 'win', axis=0, tiled=True)  117 us
    transpose x2, local copies, waits for them, and re-layouts, arrange(): moved = jnp.transpose(values, (1, 4, 2, 0, 3, 5))  22.6 us
    cos x1, other arithmetic, dft_table(): jnp.cos(angles)  16.7 us
    all_to_all x1, blocking collectives, on_device(): lax.all_to_all(whitened, 'chan', split_axis=3, concat_axis=1, tiled=True)  12.4 us
    unnamed x7, local copies, waits for them, and re-layouts  9.66 us
  transfers between devices with their start and end apart: 1, of which 1 were waited for; matrix products, arithmetic and copies ran while one was open for 0% of the time, Pallas kernels for 0%

commit v1 on v0

--- a/solution.py
+++ b/solution.py
@@ -9,6 +9,19 @@
 FREQ_LO = 64
 GROUP = 32
 EPS = 1e-06
+
+
+def bind_series_in(target):
+    b_now = jnp.concatenate(
+        lax.all_to_all(
+            jnp.stack([target for _ in range(lax.psum(1, axis_name="win"))], 0),
+            axis_name="win",
+            split_axis=0,
+            concat_axis=0,
+        ),
+        0,
+    )
+    return b_now
 
 
 def dft_table(length, first_bin, bins):
@@ -62,7 +75,7 @@
     slots = block_pairs.shape[0] // lax.axis_size("win")
     first_slot = lax.axis_index("win") * slots
     mine = lax.dynamic_slice_in_dim(block_pairs, first_slot, slots, 0)
-    direct, rotated = block_layout(lax.all_gather(banded, "win", axis=0, tiled=True), BLOCK, GROUP)
+    direct, rotated = block_layout(bind_series_in(banded), BLOCK, GROUP)
     stacked = pair_terms(direct, rotated, mine)
     slot_ids = first_slot + jnp.arange(slots, dtype=jnp.int32)
     live = (slot_ids < valid_count[0]).astype(jnp.float32)

time: 213 us -> 475 us (2.23)
  the two profiles are of different devices: /device:TPU:43 before, /device:TPU:123 now
where the time goes in v1:
time: 475 us
  waiting for transfers between devices  376 us (79%)
  local copies, waits for them, and re-layouts  44.2 us (9%)
  other arithmetic  21.8 us (5%)
  blocking collectives  12.4 us (3%)
  starting transfers between devices  11.2 us (2%)
  matrix products  5.11 us (1%)
    all_to_all x1, waiting for transfers between devices, bind_series_in(): lax.all_to_all(jnp.stack([target for _ in range(lax.psum(1, axis_name='wi...  376 us
    transpose x2, local copies, waits for them, and re-layouts, arrange(): moved = jnp.transpose(values, (1, 4, 2, 0, 3, 5))  22.6 us
    cos x1, other arithmetic, dft_table(): jnp.cos(angles)  16.7 us
    all_to_all x1, blocking collectives, on_device(): lax.all_to_all(whitened, 'chan', split_axis=3, concat_axis=1, tiled=True)  12.4 us
    all_to_all x1, starting transfers between devices, bind_series_in(): lax.all_to_all(jnp.stack([target for _ in range(lax.psum(1, axis_name='wi...  11.2 us
    unnamed x7, local copies, waits for them, and re-layouts  9.66 us
  transfers between devices with their start and end apart: 1, of which 1 were waited for; matrix products, arithmetic and copies ran while one was open for 0% of the time, Pallas kernels for 0%

profile of v1, /device:TPU:123, one launch (start us, length us, event | category | flops | bytes accessed | tf_op | source)
XLA Modules:
  0.0 474.8 jit_solution(6579077630021551596)
XLA Ops:
  0.0 0.0 copy-start
  0.0 0.0 copy-start.2
  0.0 16.7 %fusion.10 = (f32[4096,256]{1,0:T(8,128)S(1)}, f32[4096,256]{1,0:T(8,128)S(1)}) fusion(s32[256]{0:T(256)S(1)} %iota_add_fusion), kind=kLoop, calls=%fused_computation.17 | loop fusion | flops 15728640 | bytes 8389632 | tf_op jit(solution)/shard_map/cos | solution.py:33
  16.7 0.0 copy-done.2
  16.7 2.5 multiply_reduce_fusion
  19.2 0.1 fusion.14
  19.4 0.1 reshape.48
  19.5 0.8 copy.13
  20.3 12.4 %all_to_all.20 = bf16[2,256,2,256]{1,2,0,3:T(2,128)(2,1)S(1)} all-to-all(bf16[2,256,2,256]{1,2,0,3:T(2,128)(2,1)S(1)} %copy.13), channel_id=1, replica_groups=mesh['win'=32,'chan'=8] {'chan'}, dimensions={3} | all-to-all | bytes 1048576 | tf_op jit(solution)/shard_map/all_to_all | solution.py:73
  32.7 0.1 copy.14
  32.9 6.0 %stack.7 = bf16[32,2,2048,2,32]{2,4,3,1,0:T(8,128)(2,1)} broadcast(bf16[2,2048,2,32]{1,3,2,0:T(8,128)(2,1)S(1)} %bitcast.46), dimensions={1,2,3,4} | broadcast | bytes 17301504 | tf_op jit(solution)/shard_map/stack | solution.py:17
  38.8 11.2 %all-to-all-start.1 = ((bf16[32,2,2048,2,32]{2,4,3,1,0:T(8,128)(2,1)}), bf16[32,2,2048,2,32]{2,4,3,1,0:T(8,128)(2,1)}, u32[]{:S(2)}, u32[]{:S(2)}) async-start(bf16[32,2,2048,2,32]{2,4,3,1,0:T(8,128)(2,1)} %stack.7), calls=%async_computation.1 | async-start | bytes 33554432 | tf_op jit(solution)/shard_map/all_to_all | solution.py:16
  50.0 0.0 copy-done
  50.0 0.1 constant_dynamic-slice_fusion.2
  50.1 0.5 fusion.19
  54.8 375.9 %all-to-all-done.1 = bf16[32,2,2048,2,32]{2,4,3,1,0:T(8,128)(2,1)} async-done(((bf16[32,2,2048,2,32]{2,4,3,1,0:T(8,128)(2,1)}), bf16[32,2,2048,2,32]{2,4,3,1,0:T(8,128)(2,1)}, u32[]{:S(2)}, u32[]{:S(2)}) %all-to-all-start.1) | async-done | bytes 16777248 | tf_op jit(solution)/shard_map/all_to_all | solution.py:16
  430.6 9.6 %copy.21 = bf16[512,8,16,128]{3,2,1,0:T(8,128)(2,1)S(1)} copy(bf16[512,8,16,128]{3,1,2,0:T(8,128)(2,1)} %bitcast.27) | data formatting | bytes 33554432
  440.3 12.0 %copy.16 = bf16[16,1,128,64,2,32]{2,5,4,3,0,1:T(8,128)(2,1)} copy(bf16[16,1,128,64,2,32]{2,0,5,4,3,1:T(8,128)(2,1)S(1)} %bitcast.40) | data formatting | bytes 33554432 | tf_op jit(solution)/shard_map/transpose | solution.py:44
  452.3 1.7 fusion.18
  453.9 1.7 maximum_bitcast_fusion
  455.6 10.7 %copy.17 = bf16[16,1,128,64,2,32]{2,5,4,3,0,1:T(8,128)(2,1)S(1)} copy(bf16[16,1,128,64,2,32]{2,0,5,4,3,1:T(8,128)(2,1)S(1)} %maximum_bitcast_fusion) | data formatting | bytes 33554432 | tf_op jit(solution)/shard_map/transpose | solution.py:44
  466.3 1.4 constant_dynamic-slice_fusion
  467.7 0.0 copy-start.1
  467.7 1.6 pad_maximum_fusion
  469.2 2.9 copy.18
  472.2 2.6 fusion.11
  474.8 0.0 copy-done.1
  (3 shorter events, 0.1 us)
Async XLA Ops:
  0.0 50.0 %copy-start = (s32[32,2]{0,1:T(2,128)S(1)}, s32[32,2]{0,1:T(2,128)}, u32[]{:S(2)}) copy-start(s32[32,2]{0,1:T(2,128)} %param.4) | copy-start | bytes 772
  0.0 16.7 %copy-start.2 = (bf16[2,256,4096]{2,1,0:T(8,128)(2,1)S(1)}, bf16[2,256,4096]{2,1,0:T(8,128)(2,1)}, u32[]{:S(2)}) copy-start(bf16[2,256,4096]{2,1,0:T(8,128)(2,1)} %param.3) | copy-start | bytes 12582916
  38.8 391.8 %all-to-all-start.1 = ((bf16[32,2,2048,2,32]{2,4,3,1,0:T(8,128)(2,1)}), bf16[32,2,2048,2,32]{2,4,3,1,0:T(8,128)(2,1)}, u32[]{:S(2)}, u32[]{:S(2)}) async-start(bf16[32,2,2048,2,32]{2,4,3,1,0:T(8,128)(2,1)} %stack.7), calls=%async_computation.1 | async-start | bytes 33554432 | tf_op jit(solution)/shard_map/all_to_all | solution.py:16
  467.7 7.1 %copy-start.1 = (s32[32,2]{0,1:T(2,128)S(1)}, s32[32,2]{0,1:T(2,128)}, u32[]{:S(2)}) copy-start(s32[32,2]{0,1:T(2,128)} %param.4) | copy-start | bytes 772
